TPU v7x, 128 devices: a whole 4x4x4 slice. The times are simulated.
128 devices in a mesh: grp: 4 (over z), ocn: 32 (over y, x, core).
Axes of the slice: x: 4, y: 4, z: 4, core: 2. Of those that a mesh axis runs over, the one named last changes fastest.
Arguments:
- ocean_state: float32 [4, 80, 131072], P(None, None, ('grp', 'ocn')), may hold values from -6 to 6
- adv_coef: float32 [6, 131072], P(None, ('grp', 'ocn')), may hold values from 0 to 0.15
- neighbours: int32 [6, 131072], P(None, ('grp', 'ocn')), may hold values from -512 to 512, as said below
- active_levels: int32 [131072], P(('grp', 'ocn')), may hold values from 1 to 80
- boundary_level: int32 [131072], P(('grp', 'ocn')), may hold values from 1 to 80
- kpp_diff: float32 [80, 131072], P(None, ('grp', 'ocn')), may hold values from 0.3 to 30
- kpp_visc: float32 [80, 131072], P(None, ('grp', 'ocn')), may hold values from 0.3 to 30
- atm_flux: float32 [4, 262144], P(None, ('grp', 'ocn')), may hold values from -6 to 6
- pair_source: int32 [2097152], P(('grp', 'ocn')), may hold values from 0 to 2047
- pair_weight: float32 [2097152], P(('grp', 'ocn')), may hold values from 0.1 to 1
- pair_device: int32 [2097152, 1], P(('grp', 'ocn')), may hold values from 0 to 127; in each aligned block of 16384 rows (0 to 16383, 16384 to 32767, ...) at most 256 rows name the same one
- pair_cell: int32 [2097152], P(('grp', 'ocn')), may hold values from 0 to 1023
Outputs:
- ocean_after: float32 [4, 80, 131072], P(None, None, ('grp', 'ocn'))
- surface_flux: float32 [4, 131072], P(None, ('grp', 'ocn'))
Inputs may be any that keep to these rules, and one draw needn't show every extreme that they name: neighbours[k, c] is never 0. `pair_device`: among the pairs of one device, at most 256 name the same device, and some device is named exactly 256 times.
All inputs are finite; a program needn't handle non-finite values.
Results may differ from a plain program's by a relative error of at most 0.0003.
Values sent between devices are 32-bit elements; how exact they have to be, the bound alone decides.
A program may use at most 128 MiB of HBM per device.

v0:
```python
import functools

import jax
import jax.numpy as jnp
from jax import lax
from jax.experimental import pallas as pl
from jax.experimental.pallas import tpu as pltpu
from jax.sharding import PartitionSpec as P

NFIELD = 4
NEI = 6
HW = 512
ADV_STEPS = 2
SLOTS = 256
LANES = 128
SLAB = 16
USED = 10
MESH = pl.DeviceIdType.MESH
F32 = jnp.float32
BF16 = jnp.bfloat16
I32 = jnp.int32


def iota(shape, dim):
    return lax.broadcasted_iota(I32, shape, dim)


def nt_dot(a, b):
    return lax.dot_general(a, b, (((1,), (1,)), ((), ())), preferred_element_type=F32)


def pack_kernel(n, dev_ref, src_ref, cell_ref, w_ref, atm_ref, out_ref, acc, carry, tabs):
    chunk = 8
    acc[...] = jnp.zeros_like(acc)
    carry[...] = jnp.zeros_like(carry)
    ntab = atm_ref.shape[1] // LANES
    for f in range(NFIELD):
        for r in range(ntab):
            tabs[f * ntab + r] = jnp.broadcast_to(
                atm_ref[f : f + 1, r * LANES : (r + 1) * LANES], (8, LANES)
            )
    iota_d = iota((n, LANES), 0)
    iota_r = iota((SLOTS, LANES), 0).astype(F32)
    tri = jnp.where(iota((256, 256), 0) <= iota((256, 256), 1), 1.0, 0.0).astype(BF16)

    def one_chunk(i, _):
        at = pl.ds(pl.multiple_of(i * chunk, chunk), chunk)
        dest = dev_ref[at, :]
        code = src_ref[at, :] * 1024 + cell_ref[at, :]
        weight = w_ref[at, :]
        high = weight.astype(BF16).astype(F32)
        pieces = [
            (code & 127).astype(F32),
            ((code >> 7) & 127).astype(F32),
            (code >> 14).astype(F32),
            high,
            weight - high,
        ]
        run = carry[...]
        left = [[] for _ in pieces]
        right = []
        for s in range(0, chunk, 2):
            hit = [iota_d == dest[s + h : s + h + 1, :] for h in range(2)]
            member = jnp.concatenate(
                [jnp.where(m, 1.0, 0.0) for m in hit], axis=1
            ).astype(BF16)
            count = jnp.dot(member, tri, preferred_element_type=F32)
            for h in range(2):
                upto = count[:, h * LANES : (h + 1) * LANES] + run
                rank = jnp.sum(jnp.where(hit[h], upto, 0.0), axis=0, keepdims=True) - 1.0
                right.append(jnp.where(iota_r == rank, 1.0, 0.0).astype(BF16))
            run = run + jnp.broadcast_to(count[:, 255:256], (n, LANES))
            spread = member.reshape(n // 16, 16, 2 * LANES)
            for v, piece in enumerate(pieces):
                row = jnp.concatenate(
                    [
                        jnp.broadcast_to(piece[s + h : s + h + 1, :], (16, LANES))
                        for h in range(2)
                    ],
                    axis=1,
                ).astype(BF16)
                left[v].append((spread * row[None]).reshape(n, 2 * LANES))
        carry[...] = run
        lhs = jnp.concatenate([jnp.concatenate(part, axis=1) for part in left], axis=0)
        acc[...] += nt_dot(lhs, jnp.concatenate(right, axis=1))
        return 0

    lax.fori_loop(0, dev_ref.shape[0] // chunk, one_chunk, 0)

    def one_tile(t, _):
        for h in range(2):
            lanes = slice(h * LANES, (h + 1) * LANES)

            def part(v):
                return acc[pl.ds(pl.multiple_of(v * n + t * 8, 8), 8), lanes]

            code = (part(0) + part(1) * 128.0 + part(2) * 16384.0).astype(I32)
            weight = part(3) + part(4)
            cell = (code & 1023).astype(F32)
            source = code >> 10
            low = source & (LANES - 1)
            high = source >> 7
            values = [jnp.zeros((8, LANES), F32) for _ in range(NFIELD)]
            for r in range(ntab):
                here = high == r
                for f in range(NFIELD):
                    got = jnp.take_along_axis(tabs[f * ntab + r], low, axis=1)
                    values[f] = jnp.where(here, got, values[f])
            for f in range(NFIELD):
                out_ref[pl.ds(t * 8 * SLAB + f * 2 + h, 8, stride=SLAB), :] = values[f] * weight
            out_ref[pl.ds(t * 8 * SLAB + 8 + h, 8, stride=SLAB), :] = cell
        return 0

    lax.fori_loop(0, n // 8, one_tile, 0)


def move_kernel(
    n, n_inner, levels, cells,
    q_ref, coef_ref, nb_ref, act_ref, act8_ref, bl8_ref, kd_ref, kv_ref, packed_ref,
    z_ref, e_ref, r0_ref, recv_ref,
    halo, q1, split, sten_h, sten_l, rates, recip, rows,
    halo_send, halo_recv, slab_send, slab_recv, own_sem,
):
    rows_all = NFIELD * levels
    me = lax.axis_index("grp") * n_inner + lax.axis_index("ocn")

    def ident(d):
        return (d // n_inner, lax.rem(d, n_inner))

    right = lax.rem(me + 1, n)
    left = lax.rem(me + n - 1, n)
    barrier = pltpu.get_barrier_semaphore()

    def greet(i, _):
        pl.semaphore_signal(
            barrier, inc=1, device_id=ident(lax.rem(me + i, n)), device_id_type=MESH
        )
        return 0

    lax.fori_loop(1, n, greet, 0)
    pl.semaphore_wait(barrier, n - 1)

    def halo_copies(step, source):
        to_left = pltpu.make_async_remote_copy(
            src_ref=source.at[:, :, pl.ds(0, HW)],
            dst_ref=halo.at[step, 1],
            send_sem=halo_send.at[step, 0],
            recv_sem=halo_recv.at[step, 1],
            device_id=ident(left),
            device_id_type=MESH,
        )
        to_right = pltpu.make_async_remote_copy(
            src_ref=source.at[:, :, pl.ds(cells - HW, HW)],
            dst_ref=halo.at[step, 0],
            send_sem=halo_send.at[step, 1],
            recv_sem=halo_recv.at[step, 0],
            device_id=ident(right),
            device_id_type=MESH,
        )
        return to_left, to_right

    first = halo_copies(0, q_ref)
    first[0].start()
    first[1].start()

    def slab_copy(d):
        return pltpu.make_async_remote_copy(
            src_ref=packed_ref.at[pl.ds(pl.multiple_of(d * SLAB, 8), SLAB), :],
            dst_ref=recv_ref.at[pl.ds(pl.multiple_of(me * SLAB, 8), SLAB), :],
            send_sem=slab_send,
            recv_sem=slab_recv,
            device_id=ident(d),
            device_id_type=MESH,
        )

    def send_slab(i, _):
        slab_copy(lax.rem(me + i, n)).start()
        return 0

    lax.fori_loop(1, n, send_slab, 0)
    mine = pl.ds(pl.multiple_of(me * SLAB, 8), SLAB)
    own = pltpu.make_async_copy(packed_ref.at[mine, :], recv_ref.at[mine, :], own_sem)
    own.start()

    block = 256
    band = block + 2 * HW
    offset = [nb_ref[k : k + 1, :] for k in range(NEI)]
    weight = [coef_ref[k : k + 1, :] for k in range(NEI)]
    total = weight[0]
    for k in range(1, NEI):
        total = total + weight[k]
    merged = []
    for k in range(NEI):
        w = weight[k]
        for j in range(k):
            w = w + jnp.where(offset[j] == offset[k], weight[j], 0.0)
        merged.append(w)
    rows[0:1, :] = total
    local = lax.rem(iota((1, cells), 1), block) + HW
    target = [local + offset[k] for k in range(NEI)]
    for b in range(cells // block):
        cols = slice(b * block, (b + 1) * block)
        aim = [t[:, cols] for t in target]
        put = [w[:, cols] for w in merged]

        def one_band(i, _):
            at = pl.ds(pl.multiple_of(i * 128, 128), 128)
            row = iota((128, block), 0) + i * 128
            value = jnp.zeros((128, block), F32)
            for k in range(NEI):
                value = jnp.where(row == aim[k], put[k], value)
            high = value.astype(BF16)
            sten_h[b, at, :] = high
            sten_l[b, at, :] = (value - high.astype(F32)).astype(BF16)
            return 0

        lax.fori_loop(0, band // 128, one_band, 0)

    def put_split(field, lanes, value):
        high = value.astype(BF16)
        split[pl.ds(field * levels, levels), lanes] = high
        split[pl.ds(rows_all + field * levels, levels), lanes] = (
            value - high.astype(F32)
        ).astype(BF16)

    for f in range(NFIELD):
        put_split(f, pl.ds(HW, cells), q_ref[f])

    tiles = cells // LANES
    for j in range(tiles):
        lanes = slice(j * LANES, (j + 1) * LANES)
        rates[pl.ds(j, levels, stride=tiles), :] = kd_ref[:, lanes]
        rates[pl.ds(levels * tiles + j, levels, stride=tiles), :] = kv_ref[:, lanes]
    active8 = act8_ref[...]
    bound8 = bl8_ref[...]

    def one_level(i, below):
        level = levels - 1 - i
        is_open = (active8 > level) & (level >= 1)
        inside = bound8 > level
        after = []
        for c in range(2):
            at = pl.ds(pl.multiple_of((c * levels + level) * tiles, 8), tiles)
            face = jnp.where(is_open, jnp.where(inside, rates[at, :], 0.05), 0.0)
            inverse = 1.0 / (1.0 + face + below[c])
            ratio = face * inverse
            recip[at, :] = inverse
            e_ref[at, :] = ratio
            after.append(face - face * ratio)
        return tuple(after)

    nothing = jnp.zeros((tiles, LANES), F32)
    lax.fori_loop(0, levels, one_level, (nothing, nothing), unroll=4)
    for c in range(2):
        r0_ref[c * tiles : (c + 1) * tiles, :] = recip[pl.ds(c * levels * tiles, tiles), :]

    def transport(b, source):
        window = pl.ds(b * block, band)
        both = jnp.dot(split[:, window], sten_h[b], preferred_element_type=F32)
        extra = jnp.dot(split[:rows_all, window], sten_l[b], preferred_element_type=F32)
        inflow = both[:rows_all] + both[rows_all:] + extra
        cols = slice(b * block, (b + 1) * block)
        live = iota((levels, block), 0) < act_ref[:, cols]
        out = []
        for f in range(NFIELD):
            centre = source[f, :, cols]
            moved = centre + inflow[f * levels : (f + 1) * levels] - centre * rows[0:1, cols]
            out.append(jnp.where(live, moved, centre))
        return out

    nblock = cells // block
    for step in range(ADV_STEPS):
        copies = first if step == 0 else second
        for side in range(2):
            copies[1 - side].wait_recv()
            for f in range(NFIELD):
                put_split(f, pl.ds(0 if side == 0 else HW + cells, HW), halo[step, side, f])
            for b in range(side * nblock // 2, (side + 1) * nblock // 2):
                got = transport(b, q_ref if step == 0 else q1)
                for f in range(NFIELD):
                    if step == 0:
                        q1[f, :, b * block : (b + 1) * block] = got[f]
                    else:
                        for h in range(block // LANES):
                            z_ref[
                                pl.ds(f * levels * tiles + b * (block // LANES) + h, levels, stride=tiles), :
                            ] = got[f][:, h * LANES : (h + 1) * LANES]
            if step == 0:
                if side == 0:
                    second = halo_copies(1, q1)
                second[side].start()
        copies[0].wait_send()
        copies[1].wait_send()
        if step == 0:
            for f in range(NFIELD):
                put_split(f, pl.ds(HW, cells), q1[f])

    def lift(i, above):
        level = levels - 1 - i
        after = []
        for f in range(NFIELD):
            at = pl.ds(pl.multiple_of((f * levels + level) * tiles, 8), tiles)
            own_at = pl.ds(pl.multiple_of((f // 2 * levels + level) * tiles, 8), tiles)
            right_side = z_ref[at, :] + above[f]
            z_ref[at, :] = recip[own_at, :] * right_side
            after.append(e_ref[own_at, :] * right_side)
        return tuple(after)

    lax.fori_loop(0, levels, lift, (nothing,) * NFIELD, unroll=4)

    own.wait()
    everyone = pl.ds(0, (n - 1) * SLAB)
    arrived = pltpu.make_async_remote_copy(
        src_ref=packed_ref.at[everyone, :],
        dst_ref=recv_ref.at[everyone, :],
        send_sem=slab_send,
        recv_sem=slab_recv,
        device_id=ident(right),
        device_id_type=MESH,
    )
    arrived.wait_send()
    arrived.wait_recv()


def finish_kernel(n, levels, cells, z_ref, e_ref, r0_ref, recv_ref, out_ref, surface_ref, state, acc):
    tiles = cells // LANES
    group = 4
    acc[...] = jnp.zeros_like(acc)
    iota_a = iota((tiles, LANES), 0)
    iota_b = iota((LANES, LANES), 0)

    def some_slabs(i, _):
        left = [[] for _ in range(2 * NFIELD)]
        right = []
        for s in range(group):
            base = pl.multiple_of((i * group + s) * SLAB, 8)
            values = recv_ref[pl.ds(base, 8), :]
            cell = recv_ref[pl.ds(base + 8, 8), :].astype(I32)
            for h in range(2):
                at = cell[h : h + 1, :]
                hit = iota_a == (at >> 7)
                right.append(jnp.where(iota_b == (at & 127), 1.0, 0.0).astype(BF16))
                for f in range(NFIELD):
                    value = jnp.where(hit, values[f * 2 + h : f * 2 + h + 1, :], 0.0)
                    high = value.astype(BF16).astype(F32)
                    left[f].append(high)
                    left[NFIELD + f].append(value - high)
        lhs = jnp.concatenate([jnp.concatenate(part, axis=1) for part in left], axis=0)
        acc[...] += nt_dot(lhs.astype(BF16), jnp.concatenate(right, axis=1))
        return 0

    lax.fori_loop(0, n // group, some_slabs, 0)
    half = NFIELD * tiles
    below = []
    for f in range(NFIELD):
        at = pl.ds(f * tiles, tiles)
        surface = acc[at, :] + acc[pl.ds(half + f * tiles, tiles), :]
        for a in range(tiles):
            surface_ref[f : f + 1, a * LANES : (a + 1) * LANES] = surface[a : a + 1, :]
        c = f // 2
        top = z_ref[pl.ds(f * levels * tiles, tiles), :] + surface * r0_ref[c * tiles : (c + 1) * tiles, :]
        state[pl.ds(f * levels * tiles, tiles), :] = top
        below.append(top)

    def drop(level, above):
        after = []
        for f in range(NFIELD):
            at = pl.ds(pl.multiple_of((f * levels + level) * tiles, 8), tiles)
            own_at = pl.ds(pl.multiple_of((f // 2 * levels + level) * tiles, 8), tiles)
            value = z_ref[at, :] + e_ref[own_at, :] * above[f]
            state[at, :] = value
            after.append(value)
        return tuple(after)

    lax.fori_loop(1, levels, drop, tuple(below), unroll=4)
    for f in range(NFIELD):
        for j in range(tiles):
            out_ref[f, :, j * LANES : (j + 1) * LANES] = state[
                pl.ds(f * levels * tiles + j, levels, stride=tiles), :
            ]


def vmem(count):
    return [pl.BlockSpec(memory_space=pltpu.VMEM)] * count


def shaped(*shape):
    return jax.ShapeDtypeStruct(shape, F32)


def per_device(
    n, n_inner,
    ocean_state, adv_coef, neighbours, active_levels, boundary_level, kpp_diff, kpp_visc,
    atm_flux, pair_source, pair_weight, pair_device, pair_cell,
):
    levels, cells = ocean_state.shape[1:]
    tiles = cells // LANES
    pairs = pair_source.shape[0]
    wide = (pairs // LANES, LANES)
    limit = 56 * 1024 * 1024
    packed = pl.pallas_call(
        functools.partial(pack_kernel, n),
        out_shape=shaped(n * SLAB, LANES),
        in_specs=vmem(5),
        out_specs=vmem(1)[0],
        scratch_shapes=[
            pltpu.VMEM((5 * n, SLOTS), F32),
            pltpu.VMEM((n, LANES), F32),
            pltpu.VMEM((NFIELD * atm_flux.shape[1] // LANES, 8, LANES), F32),
        ],
        compiler_params=pltpu.CompilerParams(vmem_limit_bytes=limit),
        name="pack",
    )(
        pair_device.reshape(wide), pair_source.reshape(wide), pair_cell.reshape(wide),
        pair_weight.reshape(wide), atm_flux,
    )
    rows_all = NFIELD * levels
    band = 256 + 2 * HW
    z, e, r0, received = pl.pallas_call(
        functools.partial(move_kernel, n, n_inner, levels, cells),
        out_shape=(
            shaped(rows_all * tiles, LANES),
            shaped(2 * levels * tiles, LANES),
            shaped(2 * tiles, LANES),
            shaped(n * SLAB, LANES),
        ),
        in_specs=vmem(9),
        out_specs=tuple(vmem(4)),
        scratch_shapes=[
            pltpu.VMEM((ADV_STEPS, 2, NFIELD, levels, HW), F32),
            pltpu.VMEM((NFIELD, levels, cells), F32),
            pltpu.VMEM((2 * rows_all, cells + 2 * HW), BF16),
            pltpu.VMEM((cells // 256, band, 256), BF16),
            pltpu.VMEM((cells // 256, band, 256), BF16),
            pltpu.VMEM((2 * levels * tiles, LANES), F32),
            pltpu.VMEM((2 * levels * tiles, LANES), F32),
            pltpu.VMEM((8, cells), F32),
            pltpu.SemaphoreType.DMA((ADV_STEPS, 2)),
            pltpu.SemaphoreType.DMA((ADV_STEPS, 2)),
            pltpu.SemaphoreType.DMA,
            pltpu.SemaphoreType.DMA,
            pltpu.SemaphoreType.DMA,
        ],
        compiler_params=pltpu.CompilerParams(
            vmem_limit_bytes=limit, collective_id=0, has_side_effects=True
        ),
        name="move",
    )(
        ocean_state, adv_coef, neighbours, active_levels.reshape(1, cells),
        active_levels.reshape(tiles, LANES), boundary_level.reshape(tiles, LANES),
        kpp_diff, kpp_visc, packed,
    )
    return pl.pallas_call(
        functools.partial(finish_kernel, n, levels, cells),
        out_shape=(shaped(NFIELD, levels, cells), shaped(NFIELD, cells)),
        in_specs=vmem(4),
        out_specs=tuple(vmem(2)),
        scratch_shapes=[
            pltpu.VMEM((rows_all * tiles, LANES), F32),
            pltpu.VMEM((2 * NFIELD * tiles, LANES), F32),
        ],
        compiler_params=pltpu.CompilerParams(vmem_limit_bytes=limit),
        name="finish",
    )(z, e, r0, received)


def solution(mesh):
    both = ("grp", "ocn")
    placed = (
        P(None, None, both), P(None, both), P(None, both), P(both), P(both), P(None, both),
        P(None, both), P(None, both), P(both), P(both), P(both, None), P(both),
    )
    n_inner = mesh.shape["ocn"]
    return jax.shard_map(
        functools.partial(per_device, mesh.shape["grp"] * n_inner, n_inner),
        mesh=mesh,
        in_specs=placed,
        out_specs=(P(None, None, both), P(None, both)),
        check_vma=False,
    )
```

profile of v0, /device:TPU:0, one launch (start us, length us, event | category | flops | bytes accessed | tf_op | source)
XLA Modules:
  0.0 80.4 jit_solution(629914871439032666)
XLA Ops:
  0.6 19.0 %pack.1.packed_ref = f32[2048,128]{1,0:T(8,128)} custom-call(s32[128,128]{1,0:T(8,128)} %bitcast.7, s32[128,128]{1,0:T(8,128)} %bitcast.8, s32[128,128]{1,0:T(8,128)} %bitcast.9, f32[128,128]{1,0:T(8,128)} %bitcast.10, f32[4,2048]{1,0:T(4,128)} %atm_ref.1), custom_call_target="tpu_custom_call" | custom-call | tf_op jit(solution)/shard_map/pack/pallas_call | solution.py:401
  19.6 50.4 %move.1 = (f32[2560,128]{1,0:T(8,128)}, f32[1280,128]{1,0:T(8,128)}, f32[16,128]{1,0:T(8,128)}, f32[2048,128]{1,0:T(8,128)}) custom-call(f32[4,80,1024]{2,1,0:T(8,128)} %q_ref.1, f32[6,1024]{1,0:T(8,128)} %coef_ref.1, s32[6,1024]{1,0:T(8,128)} %nb_ref.1, s32[1,1024]{1,0:T(1,128)} %bitcast.11, s32[8,128]{1,0:T(8,128)} %bitcast.12, s32[8,128]{1,0:T(8,128)} %bitcast.13, ...), custom_call_target="tpu_custom_call" | custom-call | tf_op jit(solution)/shard_map/move/pallas_call | solution.py:419
  70.0 10.4 %finish.1 = (f32[4,80,1024]{2,1,0:T(8,128)}, f32[4,1024]{1,0:T(4,128)}) custom-call(f32[2560,128]{1,0:T(8,128)} %get-tuple-element.6.z_ref, f32[1280,128]{1,0:T(8,128)} %get-tuple-element.7.e_ref, f32[16,128]{1,0:T(8,128)} %get-tuple-element.8.r0_ref, f32[2048,128]{1,0:T(8,128)} %get-tuple-element.9.recv_ref), custom_call_target="tpu_custom_call" | custom-call | tf_op jit(solution)/shard_map/finish/pallas_call | solution.py:453
where the time goes:
time: 80.6 us; the launch traced here: 80.4 us
  Pallas kernels  79.8 us (99%)
    pallas_call x1, Pallas kernels, per_device(): pl.pallas_call(functools.partial(move_kernel, n, n_inner, levels, cells),...  50.4 us
    pallas_call x1, Pallas kernels, per_device(): pl.pallas_call(functools.partial(pack_kernel, n), out_shape=shaped(n * SL...  19 us
    pallas_call x1, Pallas kernels, per_device(): pl.pallas_call(functools.partial(finish_kernel, n, levels, cells), out_sh...  10.4 us

commit v1 on v0

v1 whole, which is shorter than its diff:
```python
import functools

import jax
import jax.numpy as jnp
from jax import lax
from jax.experimental import pallas as pl
from jax.experimental.pallas import tpu as pltpu
from jax.sharding import PartitionSpec as P

NFIELD = 4
NEI = 6
HW = 512
ADV_STEPS = 2
SLOTS = 256
LANES = 128
SLAB = 16
USED = 10
BLOCK = 256
BAND = BLOCK + 2 * HW
MESH = pl.DeviceIdType.MESH
F32 = jnp.float32
BF16 = jnp.bfloat16
I32 = jnp.int32


def iota(shape, dim):
    return lax.broadcasted_iota(I32, shape, dim)


def nt_dot(a, b):
    return lax.dot_general(a, b, (((1,), (1,)), ((), ())), preferred_element_type=F32)


def thick(row, count):
    sixteen = jnp.broadcast_to(row, (16, LANES)).astype(BF16)
    return jnp.broadcast_to(sixteen[None], (count // 16, 16, LANES)).reshape(count, LANES)


def rank_phase(n, dev_ref, ranks, chunk):
    iota_d = iota((n, LANES), 0)
    tri = jnp.where(iota((256, 256), 0) <= iota((256, 256), 1), 1.0, 0.0).astype(BF16)

    def some(i, run):
        at = pl.ds(pl.multiple_of(i * chunk, 8), chunk)
        dest = dev_ref[at, :]
        out = []
        for s in range(0, chunk, 2):
            hit = [iota_d == dest[s + h : s + h + 1, :] for h in range(2)]
            member = jnp.concatenate([jnp.where(m, 1.0, 0.0) for m in hit], axis=1).astype(BF16)
            count = jnp.dot(member, tri, preferred_element_type=F32)
            for h in range(2):
                upto = count[:, h * LANES : (h + 1) * LANES] + run
                out.append(jnp.sum(jnp.where(hit[h], upto, 0.0), axis=0, keepdims=True) - 1.0)
            run = run + jnp.broadcast_to(count[:, 255:256], (n, LANES))
        ranks[at, :] = jnp.concatenate(out, axis=0)
        return run

    lax.fori_loop(0, dev_ref.shape[0] // chunk, some, jnp.zeros((n, LANES), F32))


def place_phase(n, dev_ref, src_ref, cell_ref, w_ref, ranks, acc, chunk):
    one, zero = jnp.ones((), BF16), jnp.zeros((), BF16)
    iota_d = iota((n, LANES), 0).astype(F32).astype(BF16)
    iota_r = iota((SLOTS, LANES), 0).astype(F32).astype(BF16)
    acc[...] = jnp.zeros_like(acc)

    def some(i, _):
        at = pl.ds(pl.multiple_of(i * chunk, 8), chunk)
        dest = dev_ref[at, :].astype(F32)
        code = src_ref[at, :] * 1024 + cell_ref[at, :]
        weight = w_ref[at, :]
        rank = ranks[at, :]
        high = weight.astype(BF16).astype(F32)
        pieces = [
            (code & 127).astype(F32),
            ((code >> 7) & 127).astype(F32),
            (code >> 14).astype(F32),
            high,
            weight - high,
        ]
        left = [[] for _ in pieces]
        right = []
        for s in range(chunk):
            mask = iota_d == thick(dest[s : s + 1, :], n)
            right.append(jnp.where(iota_r == thick(rank[s : s + 1, :], SLOTS), one, zero))
            for v, piece in enumerate(pieces):
                left[v].append(jnp.where(mask, thick(piece[s : s + 1, :], n), zero))
        lhs = jnp.concatenate([jnp.concatenate(part, axis=1) for part in left], axis=0)
        acc[...] += nt_dot(lhs, jnp.concatenate(right, axis=1))
        return 0

    lax.fori_loop(0, dev_ref.shape[0] // chunk, some, 0)


def gather_phase(n, me, atm_ref, acc, out_ref, tabs, send):
    ntab = atm_ref.shape[1] // LANES
    tiles = 2
    trips = n // (8 * tiles)
    for f in range(NFIELD):
        for r in range(ntab):
            tabs[f * ntab + r] = jnp.broadcast_to(
                atm_ref[f : f + 1, r * LANES : (r + 1) * LANES], (8, LANES)
            )

    def some(i, _):
        turn = lax.rem(i + me // (8 * tiles), trips)
        todo = []
        for u in range(tiles):
            t = turn * tiles + u
            for h in range(2):
                lanes = slice(h * LANES, (h + 1) * LANES)

                def part(v):
                    return acc[pl.ds(pl.multiple_of(v * n + t * 8, 8), 8), lanes]

                code = (part(0) + part(1) * 128.0 + part(2) * 16384.0).astype(I32)
                weight = part(3) + part(4)
                source = code >> 10
                todo.append(
                    (t, h, weight, source & (LANES - 1), source >> 7,
                     [jnp.zeros((8, LANES), F32)] * NFIELD)
                )
                out_ref[pl.ds(t * 8 * SLAB + 8 + h, 8, stride=SLAB), :] = (code & 1023).astype(F32)
        for r in range(ntab):
            for t, h, weight, low, high, values in todo:
                here = high == r
                for f in range(NFIELD):
                    got = jnp.take_along_axis(tabs[f * ntab + r], low, axis=1)
                    values[f] = jnp.where(here, got, values[f])
        for t, h, weight, low, high, values in todo:
            for f in range(NFIELD):
                out_ref[pl.ds(t * 8 * SLAB + f * 2 + h, 8, stride=SLAB), :] = values[f] * weight

        def each(j, _):
            send(turn * 8 * tiles + lax.rem(j + me, 8 * tiles))
            return 0

        lax.fori_loop(0, 8 * tiles, each, 0)
        return 0

    lax.fori_loop(0, trips, some, 0)


def scatter_phase(n, recv_ref, acc, group):
    one, zero = jnp.ones((), BF16), jnp.zeros((), BF16)
    acc[...] = jnp.zeros_like(acc)
    iota_a = (iota((16, LANES), 0) & 7).astype(F32).astype(BF16)
    iota_b = iota((LANES, LANES), 0).astype(F32).astype(BF16)

    def some(i, _):
        left = [[] for _ in range(4)]
        right = []
        for s in range(group):
            base = pl.multiple_of((i * group + s) * SLAB, 8)
            values = recv_ref[pl.ds(base, 8), :]
            cell = recv_ref[pl.ds(base + 8, 8), :].astype(I32)
            high = values.astype(BF16).astype(F32)
            low = values - high
            major = (cell >> 7).astype(F32)
            minor = (cell & 127).astype(F32)
            for h in range(2):
                hit = iota_a == jnp.broadcast_to(major[h : h + 1, :], (16, LANES)).astype(BF16)
                right.append(jnp.where(iota_b == thick(minor[h : h + 1, :], LANES), one, zero))
                for p, piece in enumerate((high, low)):
                    for g in range(2):
                        pair = jnp.concatenate(
                            [
                                jnp.broadcast_to(piece[f * 2 + h : f * 2 + h + 1, :], (8, LANES))
                                for f in (2 * g, 2 * g + 1)
                            ],
                            axis=0,
                        ).astype(BF16)
                        left[p * 2 + g].append(jnp.where(hit, pair, zero))
        lhs = jnp.concatenate([jnp.concatenate(part, axis=1) for part in left], axis=0)
        acc[...] += nt_dot(lhs, jnp.concatenate(right, axis=1))
        return 0

    lax.fori_loop(0, n // group, some, 0)


def stencil_phase(cells, coef_ref, nb_ref, total_ref, sten_h, sten_l):
    offset = [nb_ref[k : k + 1, :] for k in range(NEI)]
    weight = [coef_ref[k : k + 1, :] for k in range(NEI)]
    total = weight[0]
    for k in range(1, NEI):
        total = total + weight[k]
    total_ref[0:1, :] = total
    merged = []
    for k in range(NEI):
        w = weight[k]
        for j in range(k):
            w = w + jnp.where(offset[j] == offset[k], weight[j], 0.0)
        merged.append(w)
    local = lax.rem(iota((1, cells), 1), BLOCK) + HW
    target = [local + offset[k] for k in range(NEI)]
    for b in range(cells // BLOCK):
        cols = slice(b * BLOCK, (b + 1) * BLOCK)
        aim = [t[:, cols] for t in target]
        put = [w[:, cols] for w in merged]

        def one_band(i, _):
            at = pl.ds(pl.multiple_of(i * 128, 128), 128)
            row = iota((128, BLOCK), 0) + i * 128
            value = jnp.zeros((128, BLOCK), F32)
            for k in range(NEI):
                value = jnp.where(row == aim[k], put[k], value)
            high = value.astype(BF16)
            sten_h[b, at, :] = high
            sten_l[b, at, :] = (value - high.astype(F32)).astype(BF16)
            return 0

        lax.fori_loop(0, BAND // 128, one_band, 0)


def move_kernel(
    n, n_inner, levels, cells,
    dev_ref, src_ref, cell_ref, w_ref, atm_ref,
    q_ref, coef_ref, nb_ref, act_ref, act8_ref, bl8_ref, kd_ref, kv_ref,
    z_ref, e_ref, r0_ref, surface_ref,
    ranks, slots, tabs, packed, received, surface_acc,
    halo, q1, split, sten_h, sten_l, rates, recip, total_ref,
    halo_send, halo_recv, slab_send, slab_recv, own_sem,
):
    tiles = cells // LANES
    me = lax.axis_index("grp") * n_inner + lax.axis_index("ocn")
    group_rows = NFIELD // 2 * levels

    def ident(d):
        return (d // n_inner, lax.rem(d, n_inner))

    barrier = pltpu.get_barrier_semaphore()

    def greet(i, _):
        pl.semaphore_signal(
            barrier, inc=1, device_id=ident(lax.rem(me + i, n)), device_id_type=MESH
        )
        return 0

    lax.fori_loop(1, n, greet, 0)
    rank_phase(n, dev_ref, ranks, 32)

    def put_split(f, lanes, value):
        g = f // 2
        at = g * 2 * group_rows + (f % 2) * levels
        high = value.astype(BF16)
        split[pl.ds(at, levels), lanes] = high
        split[pl.ds(at + group_rows, levels), lanes] = (value - high.astype(F32)).astype(BF16)

    for f in range(NFIELD):
        put_split(f, pl.ds(HW, cells), q_ref[f])
    pl.semaphore_wait(barrier, n - 1)

    far = lax.rem(me, 2)
    near = 1 - far

    def halo_copy(step, side, g):
        source = q_ref if step == 0 else q1
        fields = pl.ds(2 * g, 2)
        return pltpu.make_async_remote_copy(
            src_ref=source.at[fields, :, pl.ds(pl.multiple_of(side * HW, HW), HW)],
            dst_ref=halo.at[step, 1 - side, fields],
            send_sem=halo_send.at[step, side, g],
            recv_sem=halo_recv.at[step, 1 - side, g],
            device_id=ident(lax.rem(me + n - 1 + 2 * side, n)),
            device_id_type=MESH,
        )

    for side in (far, near):
        for g in range(2):
            halo_copy(0, side, g).start()
    place_phase(n, dev_ref, src_ref, cell_ref, w_ref, ranks, slots, 32)

    def slab_copy(d):
        return pltpu.make_async_remote_copy(
            src_ref=packed.at[pl.ds(pl.multiple_of(d * SLAB, 8), USED), :],
            dst_ref=received.at[pl.ds(pl.multiple_of(me * SLAB, 8), USED), :],
            send_sem=slab_send,
            recv_sem=slab_recv,
            device_id=ident(d),
            device_id_type=MESH,
        )

    def send_slab(d):
        @pl.when(d != me)
        def _():
            slab_copy(d).start()

    gather_phase(n, me, atm_ref, slots, packed, tabs, send_slab)
    mine = pl.ds(pl.multiple_of(me * SLAB, 8), SLAB)
    own = pltpu.make_async_copy(packed.at[mine, :], received.at[mine, :], own_sem)
    own.start()

    stencil_phase(cells, coef_ref, nb_ref, total_ref, sten_h, sten_l)

    for j in range(tiles):
        lanes = slice(j * LANES, (j + 1) * LANES)
        rates[pl.ds(j, levels, stride=tiles), :] = kd_ref[:, lanes]
        rates[pl.ds(levels * tiles + j, levels, stride=tiles), :] = kv_ref[:, lanes]
    active8 = act8_ref[...]
    bound8 = bl8_ref[...]

    def one_level(i, below):
        level = levels - 1 - i
        is_open = (active8 > level) & (level >= 1)
        inside = bound8 > level
        after = []
        for c in range(2):
            at = pl.ds(pl.multiple_of((c * levels + level) * tiles, 8), tiles)
            face = jnp.where(is_open, jnp.where(inside, rates[at, :], 0.05), 0.0)
            inverse = 1.0 / (1.0 + face + below[c])
            ratio = face * inverse
            recip[at, :] = inverse
            e_ref[at, :] = ratio
            after.append(face - face * ratio)
        return tuple(after)

    nothing = jnp.zeros((tiles, LANES), F32)
    lax.fori_loop(0, levels, one_level, (nothing, nothing), unroll=4)
    for c in range(2):
        r0_ref[c * tiles : (c + 1) * tiles, :] = recip[pl.ds(c * levels * tiles, tiles), :]

    def advance(step, side, g):
        halo_copy(step, 1 - side, g).wait_recv()
        lanes = pl.ds(pl.multiple_of(side * (HW + cells), HW), HW)
        for f in (2 * g, 2 * g + 1):
            put_split(f, lanes, halo[step, side, f])
        source = q_ref if step == 0 else q1
        at = g * 2 * group_rows
        for k in range(HW // BLOCK):
            b = side * (HW // BLOCK) + k
            cols = pl.ds(pl.multiple_of(b * BLOCK, BLOCK), BLOCK)
            window = pl.ds(pl.multiple_of(b * BLOCK, BLOCK), BAND)
            both = jnp.dot(
                split[pl.ds(at, 2 * group_rows), window], sten_h[b], preferred_element_type=F32
            )
            extra = jnp.dot(
                split[pl.ds(at, group_rows), window], sten_l[b], preferred_element_type=F32
            )
            inflow = both[:group_rows] + both[group_rows:] + extra
            live = iota((levels, BLOCK), 0) < act_ref[:, cols]
            for f in (2 * g, 2 * g + 1):
                centre = source[f, :, cols]
                moved = (
                    centre
                    + inflow[(f % 2) * levels : (f % 2 + 1) * levels]
                    - centre * total_ref[0:1, cols]
                )
                moved = jnp.where(live, moved, centre)
                if step == 0:
                    q1[f, :, cols] = moved
                else:
                    for h in range(BLOCK // LANES):
                        z_ref[
                            pl.ds(f * levels * tiles + b * (BLOCK // LANES) + h, levels, stride=tiles), :
                        ] = moved[:, h * LANES : (h + 1) * LANES]
        if step == 0:
            halo_copy(1, side, g).start()

    for side in (near, far):
        for g in range(2):
            advance(0, side, g)
    for f in range(NFIELD):
        put_split(f, pl.ds(HW, cells), q1[f])

    own.wait()
    everyone = pl.ds(0, (n - 1) * USED)
    arrived = pltpu.make_async_remote_copy(
        src_ref=packed.at[everyone, :],
        dst_ref=received.at[everyone, :],
        send_sem=slab_send,
        recv_sem=slab_recv,
        device_id=ident(lax.rem(me + 1, n)),
        device_id_type=MESH,
    )
    arrived.wait_recv()
    scatter_phase(n, received, surface_acc, 8)
    half = NFIELD * tiles
    surface_ref[...] = surface_acc[:half, :] + surface_acc[half:, :]

    for side in (near, far):
        for g in range(2):
            advance(1, side, g)

    def lift(i, above):
        level = levels - 1 - i
        after = []
        for f in range(NFIELD):
            at = pl.ds(pl.multiple_of((f * levels + level) * tiles, 8), tiles)
            own_at = pl.ds(pl.multiple_of((f // 2 * levels + level) * tiles, 8), tiles)
            right_side = z_ref[at, :] + above[f]
            z_ref[at, :] = recip[own_at, :] * right_side
            after.append(e_ref[own_at, :] * right_side)
        return tuple(after)

    lax.fori_loop(0, levels, lift, (nothing,) * NFIELD, unroll=4)
    arrived.wait_send()
    for step in range(ADV_STEPS):
        for side in range(2):
            for g in range(2):
                halo_copy(step, side, g).wait_send()


def finish_kernel(levels, cells, z_ref, e_ref, r0_ref, flux_ref, out_ref, surface_ref, state):
    tiles = cells // LANES
    below = []
    for f in range(NFIELD):
        surface = flux_ref[f * tiles : (f + 1) * tiles, :]
        for a in range(tiles):
            surface_ref[f : f + 1, a * LANES : (a + 1) * LANES] = surface[a : a + 1, :]
        c = f // 2
        top = z_ref[pl.ds(f * levels * tiles, tiles), :] + surface * r0_ref[c * tiles : (c + 1) * tiles, :]
        state[pl.ds(f * levels * tiles, tiles), :] = top
        below.append(top)

    def drop(level, above):
        after = []
        for f in range(NFIELD):
            at = pl.ds(pl.multiple_of((f * levels + level) * tiles, 8), tiles)
            own_at = pl.ds(pl.multiple_of((f // 2 * levels + level) * tiles, 8), tiles)
            value = z_ref[at, :] + e_ref[own_at, :] * above[f]
            state[at, :] = value
            after.append(value)
        return tuple(after)

    lax.fori_loop(1, levels, drop, tuple(below), unroll=4)
    for f in range(NFIELD):
        for j in range(tiles):
            out_ref[f, :, j * LANES : (j + 1) * LANES] = state[
                pl.ds(f * levels * tiles + j, levels, stride=tiles), :
            ]


def vmem(count):
    return [pl.BlockSpec(memory_space=pltpu.VMEM)] * count


def shaped(*shape):
    return jax.ShapeDtypeStruct(shape, F32)


def per_device(
    n, n_inner,
    ocean_state, adv_coef, neighbours, active_levels, boundary_level, kpp_diff, kpp_visc,
    atm_flux, pair_source, pair_weight, pair_device, pair_cell,
):
    levels, cells = ocean_state.shape[1:]
    tiles = cells // LANES
    pairs = pair_source.shape[0]
    wide = (pairs // LANES, LANES)
    rows_all = NFIELD * levels
    z, e, r0, flux = pl.pallas_call(
        functools.partial(move_kernel, n, n_inner, levels, cells),
        out_shape=(
            shaped(rows_all * tiles, LANES),
            shaped(2 * levels * tiles, LANES),
            shaped(2 * tiles, LANES),
            shaped(NFIELD * tiles, LANES),
        ),
        in_specs=vmem(13),
        out_specs=tuple(vmem(4)),
        scratch_shapes=[
            pltpu.VMEM(wide, F32),
            pltpu.VMEM((5 * n, SLOTS), F32),
            pltpu.VMEM((NFIELD * atm_flux.shape[1] // LANES, 8, LANES), F32),
            pltpu.VMEM((n * SLAB, LANES), F32),
            pltpu.VMEM((n * SLAB, LANES), F32),
            pltpu.VMEM((2 * NFIELD * tiles, LANES), F32),
            pltpu.VMEM((ADV_STEPS, 2, NFIELD, levels, HW), F32),
            pltpu.VMEM((NFIELD, levels, cells), F32),
            pltpu.VMEM((2 * rows_all, cells + 2 * HW), BF16),
            pltpu.VMEM((cells // BLOCK, BAND, BLOCK), BF16),
            pltpu.VMEM((cells // BLOCK, BAND, BLOCK), BF16),
            pltpu.VMEM((2 * levels * tiles, LANES), F32),
            pltpu.VMEM((2 * levels * tiles, LANES), F32),
            pltpu.VMEM((8, cells), F32),
            pltpu.SemaphoreType.DMA((ADV_STEPS, 2, 2)),
            pltpu.SemaphoreType.DMA((ADV_STEPS, 2, 2)),
            pltpu.SemaphoreType.DMA,
            pltpu.SemaphoreType.DMA,
            pltpu.SemaphoreType.DMA,
        ],
        compiler_params=pltpu.CompilerParams(
            vmem_limit_bytes=48 * 1024 * 1024, collective_id=0, has_side_effects=True
        ),
        name="move",
    )(
        pair_device.reshape(wide), pair_source.reshape(wide), pair_cell.reshape(wide),
        pair_weight.reshape(wide), atm_flux,
        ocean_state, adv_coef, neighbours, active_levels.reshape(1, cells),
        active_levels.reshape(tiles, LANES), boundary_level.reshape(tiles, LANES),
        kpp_diff, kpp_visc,
    )
    return pl.pallas_call(
        functools.partial(finish_kernel, levels, cells),
        out_shape=(shaped(NFIELD, levels, cells), shaped(NFIELD, cells)),
        in_specs=vmem(4),
        out_specs=tuple(vmem(2)),
        scratch_shapes=[pltpu.VMEM((rows_all * tiles, LANES), F32)],
        compiler_params=pltpu.CompilerParams(vmem_limit_bytes=32 * 1024 * 1024),
        name="finish",
    )(z, e, r0, flux)


def solution(mesh):
    both = ("grp", "ocn")
    placed = (
        P(None, None, both), P(None, both), P(None, both), P(both), P(both), P(None, both),
        P(None, both), P(None, both), P(both), P(both), P(both, None), P(both),
    )
    n_inner = mesh.shape["ocn"]
    return jax.shard_map(
        functools.partial(per_device, mesh.shape["grp"] * n_inner, n_inner),
        mesh=mesh,
        in_specs=placed,
        out_specs=(P(None, None, both), P(None, both)),
        check_vma=False,
    )
```

time: 80.6 us -> 56.7 us (0.70)
  Pallas kernels: 79.8 us -> 45.1 us
  local copies, waits for them, and re-layouts: 0 us -> 10.3 us
    pallas_call x2 -> x1, Pallas kernels: 29.3 us -> 1.57 us  [per_device(): pl.pallas_call(functools.partial(finish_kernel, levels, cells), out_shape...]
    unnamed x0 -> x24, local copies, waits for them, and re-layouts: none -> 10.3 us
    pallas_call x1, Pallas kernels: 50.4 us -> 43.5 us  [per_device(): pl.pallas_call(functools.partial(move_kernel, n, n_inner, levels, cells),...]
where the time goes in v1:
time: 56.7 us; the launch traced here: 56 us
  Pallas kernels  45.1 us (80%)
  local copies, waits for them, and re-layouts  10.3 us (18%)
  between operations  0.66 us (1%)
    pallas_call x1, Pallas kernels, per_device(): pl.pallas_call(functools.partial(move_kernel, n, n_inner, levels, cells),...  43.5 us
    unnamed x24, local copies, waits for them, and re-layouts  10.3 us
    pallas_call x1, Pallas kernels, per_device(): pl.pallas_call(functools.partial(finish_kernel, levels, cells), out_shape...  1.57 us

profile of v1, /device:TPU:0, one launch (start us, length us, event | category | flops | bytes accessed | tf_op | source)
XLA Modules:
  0.0 56.0 jit_solution(5211967969101103836)
XLA Ops:
  0.6 0.0 copy-start
  0.6 1.3 %copy-done = f32[4,80,1024]{2,1,0:T(8,128)S(1)} copy-done((f32[4,80,1024]{2,1,0:T(8,128)S(1)}, f32[4,80,1024]{2,1,0:T(8,128)}, u32[]{:S(2)}) %copy-start) | copy-done | bytes 1310744
  2.0 0.0 copy-start.1
  2.0 1.0 %copy-done.1 = f32[80,1024]{1,0:T(8,128)S(1)} copy-done((f32[80,1024]{1,0:T(8,128)S(1)}, f32[80,1024]{1,0:T(8,128)}, u32[]{:S(2)}) %copy-start.1) | copy-done | bytes 327704
  2.9 0.0 copy-start.2
  2.9 1.0 %copy-done.2 = f32[80,1024]{1,0:T(8,128)S(1)} copy-done((f32[80,1024]{1,0:T(8,128)S(1)}, f32[80,1024]{1,0:T(8,128)}, u32[]{:S(2)}) %copy-start.2) | copy-done | bytes 327704
  3.9 0.0 copy-start.3
  3.9 0.8 %copy-done.3 = s32[16384,1]{0,1:T(1,128)S(1)} copy-done((s32[16384,1]{0,1:T(1,128)S(1)}, s32[16384,1]{0,1:T(1,128)}, u32[]{:S(2)}) %copy-start.3) | copy-done | bytes 65560
  4.7 0.0 copy-start.4
  4.7 0.8 %copy-done.4 = s32[16384]{0:T(1024)S(1)} copy-done((s32[16384]{0:T(1024)S(1)}, s32[16384]{0:T(1024)}, u32[]{:S(2)}) %copy-start.4) | copy-done | bytes 65560
  5.6 0.0 copy-start.5
  5.6 0.8 %copy-done.5 = s32[16384]{0:T(1024)S(1)} copy-done((s32[16384]{0:T(1024)S(1)}, s32[16384]{0:T(1024)}, u32[]{:S(2)}) %copy-start.5) | copy-done | bytes 65560
  6.4 0.0 copy-start.6
  6.4 0.8 %copy-done.6 = f32[16384]{0:T(1024)S(1)} copy-done((f32[16384]{0:T(1024)S(1)}, f32[16384]{0:T(1024)}, u32[]{:S(2)}) %copy-start.6) | copy-done | bytes 65560
  7.3 0.0 copy-start.7
  7.3 0.8 %copy-done.7 = f32[4,2048]{1,0:T(4,128)S(1)} copy-done((f32[4,2048]{1,0:T(4,128)S(1)}, f32[4,2048]{1,0:T(4,128)}, u32[]{:S(2)}) %copy-start.7) | copy-done | bytes 32792
  8.0 0.0 copy-start.8
  8.0 0.8 %copy-done.8 = f32[6,1024]{1,0:T(8,128)S(1)} copy-done((f32[6,1024]{1,0:T(8,128)S(1)}, f32[6,1024]{1,0:T(8,128)}, u32[]{:S(2)}) %copy-start.8) | copy-done | bytes 24600
  8.8 0.0 copy-start.9
  8.8 0.8 %copy-done.9 = s32[6,1024]{1,0:T(8,128)S(1)} copy-done((s32[6,1024]{1,0:T(8,128)S(1)}, s32[6,1024]{1,0:T(8,128)}, u32[]{:S(2)}) %copy-start.9) | copy-done | bytes 24600
  9.5 0.7 %copy-done.10 = s32[1024]{0:T(1024)S(1)} copy-done((s32[1024]{0:T(1024)S(1)}, s32[1024]{0:T(1024)}, u32[]{:S(2)}) %copy-start.10) | copy-done | bytes 4120
  10.2 0.7 %copy-done.11 = s32[1024]{0:T(1024)S(1)} copy-done((s32[1024]{0:T(1024)S(1)}, s32[1024]{0:T(1024)}, u32[]{:S(2)}) %copy-start.11) | copy-done | bytes 4120
  10.9 43.5 %move.1 = (f32[2560,128]{1,0:T(8,128)S(1)}, f32[1280,128]{1,0:T(8,128)S(1)}, f32[16,128]{1,0:T(8,128)S(1)}, f32[32,128]{1,0:T(8,128)S(1)}) custom-call(s32[128,128]{1,0:T(8,128)S(1)} %bitcast.7, s32[128,128]{1,0:T(8,128)S(1)} %bitcast.8, s32[128,128]{1,0:T(8,128)S(1)} %bitcast.9, f32[128,128]{1,0:T(8,128)S(1)} %bitcast.10, f32[4,2048]{1,0:T(4,128)S(1)} %copy-done.7, ...), custom_call_target="tpu_custom_call" | custom-call | tf_op jit(solution)/shard_map/move/pallas_call | solution.py:451
  54.5 1.6 %finish.1 = (f32[4,80,1024]{2,1,0:T(8,128)}, f32[4,1024]{1,0:T(4,128)}) custom-call(f32[2560,128]{1,0:T(8,128)S(1)} %get-tuple-element.6.z_ref, f32[1280,128]{1,0:T(8,128)S(1)} %get-tuple-element.7.e_ref, f32[16,128]{1,0:T(8,128)S(1)} %get-tuple-element.8.r0_ref, f32[32,128]{1,0:T(8,128)S(1)} %get-tuple-element.9.flux_ref), custom_call_target="tpu_custom_call" | custom-call | tf_op jit(solution)/shard_map/finish/pallas_call | solution.py:493
  (2 shorter events, 0.0 us)
Async XLA Ops:
  0.6 1.3 %copy-start = (f32[4,80,1024]{2,1,0:T(8,128)S(1)}, f32[4,80,1024]{2,1,0:T(8,128)}, u32[]{:S(2)}) copy-start(f32[4,80,1024]{2,1,0:T(8,128)} %q_ref.1) | copy-start | bytes 3932164
  2.0 1.0 %copy-start.1 = (f32[80,1024]{1,0:T(8,128)S(1)}, f32[80,1024]{1,0:T(8,128)}, u32[]{:S(2)}) copy-start(f32[80,1024]{1,0:T(8,128)} %kd_ref.1) | copy-start | bytes 983044
  2.9 1.0 %copy-start.2 = (f32[80,1024]{1,0:T(8,128)S(1)}, f32[80,1024]{1,0:T(8,128)}, u32[]{:S(2)}) copy-start(f32[80,1024]{1,0:T(8,128)} %kv_ref.1) | copy-start | bytes 983044
  3.9 0.8 %copy-start.3 = (s32[16384,1]{0,1:T(1,128)S(1)}, s32[16384,1]{0,1:T(1,128)}, u32[]{:S(2)}) copy-start(s32[16384,1]{0,1:T(1,128)} %param.22) | copy-start | bytes 196612
  4.7 0.8 %copy-start.4 = (s32[16384]{0:T(1024)S(1)}, s32[16384]{0:T(1024)}, u32[]{:S(2)}) copy-start(s32[16384]{0:T(1024)} %param.20) | copy-start | bytes 196612
  5.6 0.8 %copy-start.5 = (s32[16384]{0:T(1024)S(1)}, s32[16384]{0:T(1024)}, u32[]{:S(2)}) copy-start(s32[16384]{0:T(1024)} %param.23) | copy-start | bytes 196612
  6.4 0.8 %copy-start.6 = (f32[16384]{0:T(1024)S(1)}, f32[16384]{0:T(1024)}, u32[]{:S(2)}) copy-start(f32[16384]{0:T(1024)} %param.21) | copy-start | bytes 196612
  7.3 0.8 %copy-start.7 = (f32[4,2048]{1,0:T(4,128)S(1)}, f32[4,2048]{1,0:T(4,128)}, u32[]{:S(2)}) copy-start(f32[4,2048]{1,0:T(4,128)} %atm_ref.1) | copy-start | bytes 98308
  8.0 0.8 %copy-start.8 = (f32[6,1024]{1,0:T(8,128)S(1)}, f32[6,1024]{1,0:T(8,128)}, u32[]{:S(2)}) copy-start(f32[6,1024]{1,0:T(8,128)} %coef_ref.1) | copy-start | bytes 73732
  8.8 0.8 %copy-start.9 = (s32[6,1024]{1,0:T(8,128)S(1)}, s32[6,1024]{1,0:T(8,128)}, u32[]{:S(2)}) copy-start(s32[6,1024]{1,0:T(8,128)} %nb_ref.1) | copy-start | bytes 73732
  9.5 0.7 %copy-start.10 = (s32[1024]{0:T(1024)S(1)}, s32[1024]{0:T(1024)}, u32[]{:S(2)}) copy-start(s32[1024]{0:T(1024)} %param.15) | copy-start | bytes 12292
  10.2 0.7 %copy-start.11 = (s32[1024]{0:T(1024)S(1)}, s32[1024]{0:T(1024)}, u32[]{:S(2)}) copy-start(s32[1024]{0:T(1024)} %param.16) | copy-start | bytes 12292

commit v2 on v1

--- a/solution.py
+++ b/solution.py
@@ -214,12 +214,15 @@
 
 def move_kernel(
     n, n_inner, levels, cells,
+    dev_hbm, src_hbm, cell_hbm, w_hbm, atm_hbm,
+    q_hbm, coef_hbm, nb_hbm, act_hbm, act8_hbm, bl8_hbm, kd_hbm, kv_hbm,
+    out_ref, surface_ref,
+    z_ref, e_ref, out_vmem,
     dev_ref, src_ref, cell_ref, w_ref, atm_ref,
     q_ref, coef_ref, nb_ref, act_ref, act8_ref, bl8_ref, kd_ref, kv_ref,
-    z_ref, e_ref, r0_ref, surface_ref,
     ranks, slots, tabs, packed, received, surface_acc,
     halo, q1, split, sten_h, sten_l, rates, recip, total_ref,
-    halo_send, halo_recv, slab_send, slab_recv, own_sem,
+    halo_send, halo_recv, slab_send, slab_recv, own_sem, load_sem, out_sem,
 ):
     tiles = cells // LANES
     me = lax.axis_index("grp") * n_inner + lax.axis_index("ocn")
@@ -236,7 +239,21 @@
         )
         return 0
 
-    lax.fori_loop(1, n, greet, 0)
+    loads = [
+        pltpu.make_async_copy(source, target, load_sem.at[i])
+        for i, (source, target) in enumerate(
+            [
+                (dev_hbm, dev_ref), (q_hbm, q_ref), (src_hbm, src_ref), (cell_hbm, cell_ref),
+                (w_hbm, w_ref), (atm_hbm, atm_ref), (coef_hbm, coef_ref), (nb_hbm, nb_ref),
+                (act_hbm, act_ref), (act8_hbm, act8_ref), (bl8_hbm, bl8_ref), (kd_hbm, kd_ref),
+                (kv_hbm, kv_ref),
+            ]
+        )
+    ]
+    for load in loads:
+        load.start()
+    lax.fori_loop(1, n, greet, 0, unroll=8)
+    loads[0].wait()
     rank_phase(n, dev_ref, ranks, 32)
 
     def put_split(f, lanes, value):
@@ -246,6 +263,7 @@
         split[pl.ds(at, levels), lanes] = high
         split[pl.ds(at + group_rows, levels), lanes] = (value - high.astype(F32)).astype(BF16)
 
+    loads[1].wait()
     for f in range(NFIELD):
         put_split(f, pl.ds(HW, cells), q_ref[f])
     pl.semaphore_wait(barrier, n - 1)
@@ -268,6 +286,8 @@
     for side in (far, near):
         for g in range(2):
             halo_copy(0, side, g).start()
+    for load in loads[2:]:
+        load.wait()
     place_phase(n, dev_ref, src_ref, cell_ref, w_ref, ranks, slots, 32)
 
     def slab_copy(d):
@@ -291,33 +311,6 @@
     own.start()
 
     stencil_phase(cells, coef_ref, nb_ref, total_ref, sten_h, sten_l)
-
-    for j in range(tiles):
-        lanes = slice(j * LANES, (j + 1) * LANES)
-        rates[pl.ds(j, levels, stride=tiles), :] = kd_ref[:, lanes]
-        rates[pl.ds(levels * tiles + j, levels, stride=tiles), :] = kv_ref[:, lanes]
-    active8 = act8_ref[...]
-    bound8 = bl8_ref[...]
-
-    def one_level(i, below):
-        level = levels - 1 - i
-        is_open = (active8 > level) & (level >= 1)
-        inside = bound8 > level
-        after = []
-        for c in range(2):
-            at = pl.ds(pl.multiple_of((c * levels + level) * tiles, 8), tiles)
-            face = jnp.where(is_open, jnp.where(inside, rates[at, :], 0.05), 0.0)
-            inverse = 1.0 / (1.0 + face + below[c])
-            ratio = face * inverse
-            recip[at, :] = inverse
-            e_ref[at, :] = ratio
-            after.append(face - face * ratio)
-        return tuple(after)
-
-    nothing = jnp.zeros((tiles, LANES), F32)
-    lax.fori_loop(0, levels, one_level, (nothing, nothing), unroll=4)
-    for c in range(2):
-        r0_ref[c * tiles : (c + 1) * tiles, :] = recip[pl.ds(c * levels * tiles, tiles), :]
 
     def advance(step, side, g):
         halo_copy(step, 1 - side, g).wait_recv()
@@ -362,6 +355,34 @@
     for f in range(NFIELD):
         put_split(f, pl.ds(HW, cells), q1[f])
 
+    for j in range(tiles):
+        lanes = slice(j * LANES, (j + 1) * LANES)
+        rates[pl.ds(j, levels, stride=tiles), :] = kd_ref[:, lanes]
+        rates[pl.ds(levels * tiles + j, levels, stride=tiles), :] = kv_ref[:, lanes]
+    active8 = act8_ref[...]
+    bound8 = bl8_ref[...]
+
+    def one_level(i, below):
+        level = levels - 1 - i
+        is_open = (active8 > level) & (level >= 1)
+        inside = bound8 > level
+        after = []
+        for c in range(2):
+            at = pl.ds(pl.multiple_of((c * levels + level) * tiles, 8), tiles)
+            face = jnp.where(is_open, jnp.where(inside, rates[at, :], 0.05), 0.0)
+            inverse = 1.0 / (1.0 + face + below[c])
+            ratio = face * inverse
+            recip[at, :] = inverse
+            e_ref[at, :] = ratio
+            after.append(face - face * ratio)
+        return tuple(after)
+
+    nothing = jnp.zeros((tiles, LANES), F32)
+    lax.fori_loop(0, levels, one_level, (nothing, nothing), unroll=4)
+
+    for g in range(2):
+        advance(1, near, g)
+
     own.wait()
     everyone = pl.ds(0, (n - 1) * USED)
     arrived = pltpu.make_async_remote_copy(
@@ -373,61 +394,68 @@
         device_id_type=MESH,
     )
     arrived.wait_recv()
-    scatter_phase(n, received, surface_acc, 8)
+    scatter_phase(n, received, surface_acc, 16)
     half = NFIELD * tiles
-    surface_ref[...] = surface_acc[:half, :] + surface_acc[half:, :]
-
-    for side in (near, far):
-        for g in range(2):
-            advance(1, side, g)
-
-    def lift(i, above):
-        level = levels - 1 - i
-        after = []
-        for f in range(NFIELD):
-            at = pl.ds(pl.multiple_of((f * levels + level) * tiles, 8), tiles)
-            own_at = pl.ds(pl.multiple_of((f // 2 * levels + level) * tiles, 8), tiles)
-            right_side = z_ref[at, :] + above[f]
-            z_ref[at, :] = recip[own_at, :] * right_side
-            after.append(e_ref[own_at, :] * right_side)
-        return tuple(after)
-
-    lax.fori_loop(0, levels, lift, (nothing,) * NFIELD, unroll=4)
+    surface = surface_acc[:half, :] + surface_acc[half:, :]
+    surface_acc[:half, :] = surface
+    for f in range(NFIELD):
+        for a in range(tiles):
+            r = f * tiles + a
+            surface_ref[f : f + 1, a * LANES : (a + 1) * LANES] = surface[r : r + 1, :]
+
+
+    def out_copy(g):
+        fields = pl.ds(2 * g, 2)
+        return pltpu.make_async_copy(out_vmem.at[fields], out_ref.at[fields], out_sem.at[g])
+
+    for g in range(2):
+        advance(1, far, g)
+        fields = (2 * g, 2 * g + 1)
+
+        def lift(i, above):
+            level = levels - 1 - i
+            own_at = pl.ds(pl.multiple_of((g * levels + level) * tiles, 8), tiles)
+            after = []
+            for f, carried in zip(fields, above):
+                at = pl.ds(pl.multiple_of((f * levels + level) * tiles, 8), tiles)
+                right_side = z_ref[at, :] + carried
+                z_ref[at, :] = recip[own_at, :] * right_side
+                after.append(e_ref[own_at, :] * right_side)
+            return tuple(after)
+
+        lax.fori_loop(0, levels, lift, (nothing,) * 2, unroll=8)
+        below = []
+        for f in fields:
+            at = pl.ds(f * levels * tiles, tiles)
+            flux = surface_acc[f * tiles : (f + 1) * tiles, :]
+            top = z_ref[at, :] + flux * recip[pl.ds(g * levels * tiles, tiles), :]
+            z_ref[at, :] = top
+            below.append(top)
+
+        def drop(level, above):
+            own_at = pl.ds(pl.multiple_of((g * levels + level) * tiles, 8), tiles)
+            after = []
+            for f, carried in zip(fields, above):
+                at = pl.ds(pl.multiple_of((f * levels + level) * tiles, 8), tiles)
+                value = z_ref[at, :] + e_ref[own_at, :] * carried
+                z_ref[at, :] = value
+                after.append(value)
+            return tuple(after)
+
+        lax.fori_loop(1, levels, drop, tuple(below), unroll=8)
+        for f in fields:
+            for j in range(tiles):
+                out_vmem[f, :, j * LANES : (j + 1) * LANES] = z_ref[
+                    pl.ds(f * levels * tiles + j, levels, stride=tiles), :
+                ]
+        out_copy(g).start()
+    for g in range(2):
+        out_copy(g).wait()
     arrived.wait_send()
     for step in range(ADV_STEPS):
         for side in range(2):
             for g in range(2):
                 halo_copy(step, side, g).wait_send()
-
-
-def finish_kernel(levels, cells, z_ref, e_ref, r0_ref, flux_ref, out_ref, surface_ref, state):
-    tiles = cells // LANES
-    below = []
-    for f in range(NFIELD):
-        surface = flux_ref[f * tiles : (f + 1) * tiles, :]
-        for a in range(tiles):
-            surface_ref[f : f + 1, a * LANES : (a + 1) * LANES] = surface[a : a + 1, :]
-        c = f // 2
-        top = z_ref[pl.ds(f * levels * tiles, tiles), :] + surface * r0_ref[c * tiles : (c + 1) * tiles, :]
-        state[pl.ds(f * levels * tiles, tiles), :] = top
-        below.append(top)
-
-    def drop(level, above):
-        after = []
-        for f in range(NFIELD):
-            at = pl.ds(pl.multiple_of((f * levels + level) * tiles, 8), tiles)
-            own_at = pl.ds(pl.multiple_of((f // 2 * levels + level) * tiles, 8), tiles)
-            value = z_ref[at, :] + e_ref[own_at, :] * above[f]
-            state[at, :] = value
-            after.append(value)
-        return tuple(after)
-
-    lax.fori_loop(1, levels, drop, tuple(below), unroll=4)
-    for f in range(NFIELD):
-        for j in range(tiles):
-            out_ref[f, :, j * LANES : (j + 1) * LANES] = state[
-                pl.ds(f * levels * tiles + j, levels, stride=tiles), :
-            ]
 
 
 def vmem(count):
@@ -448,17 +476,28 @@
     pairs = pair_source.shape[0]
     wide = (pairs // LANES, LANES)
     rows_all = NFIELD * levels
-    z, e, r0, flux = pl.pallas_call(
+    return pl.pallas_call(
         functools.partial(move_kernel, n, n_inner, levels, cells),
-        out_shape=(
-            shaped(rows_all * tiles, LANES),
-            shaped(2 * levels * tiles, LANES),
-            shaped(2 * tiles, LANES),
-            shaped(NFIELD * tiles, LANES),
-        ),
-        in_specs=vmem(13),
-        out_specs=tuple(vmem(4)),
+        out_shape=(shaped(NFIELD, levels, cells), shaped(NFIELD, cells)),
+        in_specs=[pl.BlockSpec(memory_space=pltpu.HBM)] * 13,
+        out_specs=(pl.BlockSpec(memory_space=pltpu.HBM), vmem(1)[0]),
         scratch_shapes=[
+            pltpu.VMEM((rows_all * tiles, LANES), F32),
+            pltpu.VMEM((2 * levels * tiles, LANES), F32),
+            pltpu.VMEM((NFIELD, levels, cells), F32),
+            pltpu.VMEM(wide, I32),
+            pltpu.VMEM(wide, I32),
+            pltpu.VMEM(wide, I32),
+            pltpu.VMEM(wide, F32),
+            pltpu.VMEM(atm_flux.shape, F32),
+            pltpu.VMEM((NFIELD, levels, cells), F32),
+            pltpu.VMEM((NEI, cells), F32),
+            pltpu.VMEM((NEI, cells), I32),
+            pltpu.VMEM((1, cells), I32),
+            pltpu.VMEM((tiles, LANES), I32),
+            pltpu.VMEM((tiles, LANES), I32),
+            pltpu.VMEM((levels, cells), F32),
+            pltpu.VMEM((levels, cells), F32),
             pltpu.VMEM(wide, F32),
             pltpu.VMEM((5 * n, SLOTS), F32),
             pltpu.VMEM((NFIELD * atm_flux.shape[1] // LANES, 8, LANES), F32),
@@ -478,9 +517,11 @@
             pltpu.SemaphoreType.DMA,
             pltpu.SemaphoreType.DMA,
             pltpu.SemaphoreType.DMA,
+            pltpu.SemaphoreType.DMA((13,)),
+            pltpu.SemaphoreType.DMA((2,)),
         ],
         compiler_params=pltpu.CompilerParams(
-            vmem_limit_bytes=48 * 1024 * 1024, collective_id=0, has_side_effects=True
+            vmem_limit_bytes=63 * 1024 * 1024, collective_id=0, has_side_effects=True
         ),
         name="move",
     )(
@@ -490,15 +531,6 @@
         active_levels.reshape(tiles, LANES), boundary_level.reshape(tiles, LANES),
         kpp_diff, kpp_visc,
     )
-    return pl.pallas_call(
-        functools.partial(finish_kernel, levels, cells),
-        out_shape=(shaped(NFIELD, levels, cells), shaped(NFIELD, cells)),
-        in_specs=vmem(4),
-        out_specs=tuple(vmem(2)),
-        scratch_shapes=[pltpu.VMEM((rows_all * tiles, LANES), F32)],
-        compiler_params=pltpu.CompilerParams(vmem_limit_bytes=32 * 1024 * 1024),
-        name="finish",
-    )(z, e, r0, flux)
 
 
 def solution(mesh):

time: 56.7 us -> 47.5 us (0.84)
  local copies, waits for them, and re-layouts: 10.3 us -> 3.14 us
  Pallas kernels: 45.1 us -> 43.6 us
    unnamed x24 -> x4, local copies, waits for them, and re-layouts: 10.3 us -> 3.14 us
    pallas_call x1 -> x0, Pallas kernels: 1.57 us -> none  [per_device(): pl.pallas_call(functools.partial(finish_kernel, levels, cells), out_shape...]
where the time goes in v2:
time: 47.5 us; the launch traced here: 47.4 us
  Pallas kernels  43.6 us (92%)
  local copies, waits for them, and re-layouts  3.14 us (7%)
  between operations  0.65 us (1%)
    pallas_call x1, Pallas kernels, per_device(): pl.pallas_call(functools.partial(move_kernel, n, n_inner, levels, cells),...  43.6 us
    unnamed x4, local copies, waits for them, and re-layouts  3.14 us

profile of v2, /device:TPU:0, one launch (start us, length us, event | category | flops | bytes accessed | tf_op | source)
XLA Modules:
  0.0 47.4 jit_solution(4366506268714670782)
XLA Ops:
  0.6 43.6 %move.1 = (f32[4,80,1024]{2,1,0:T(8,128)}, f32[4,1024]{1,0:T(4,128)}) custom-call(s32[128,128]{1,0:T(8,128)} %bitcast.7, s32[128,128]{1,0:T(8,128)} %bitcast.8, s32[128,128]{1,0:T(8,128)} %bitcast.9, f32[128,128]{1,0:T(8,128)} %bitcast.10, f32[4,2048]{1,0:T(4,128)} %atm_hbm.1, f32[4,80,1024]{2,1,0:T(8,128)} %q_hbm.1, f32[6,1024]{1,0:T(8,128)} %coef_hbm.1, ...), custom_call_target="tpu_custom_call" | custom-call | tf_op jit(solution)/shard_map/move/pallas_call | solution.py:479
  44.2 0.0 copy-start
  44.3 2.5 %copy.16 = f32[4,80,1024]{2,1,0:T(8,128)} copy(f32[4,80,1024]{2,1,0:T(8,128)} %get-tuple-element.4) | data formatting | bytes 2621440
  46.8 0.0 copy-done
  46.8 0.6 %copy.17 = f32[4,1024]{1,0:T(4,128)} copy(f32[4,1024]{1,0:T(4,128)S(1)} %copy-done) | data formatting | bytes 32768
Async XLA Ops:
  44.2 2.5 %copy-start = (f32[4,1024]{1,0:T(4,128)S(1)}, f32[4,1024]{1,0:T(4,128)}, u32[]{:S(2)}) copy-start(f32[4,1024]{1,0:T(4,128)} %get-tuple-element.5) | copy-start | bytes 49156

commit v3 on v2

--- a/solution.py
+++ b/solution.py
@@ -92,10 +92,12 @@
     lax.fori_loop(0, dev_ref.shape[0] // chunk, some, 0)
 
 
-def gather_phase(n, me, atm_ref, acc, out_ref, tabs, send):
+def gather_phase(n, n_inner, me, atm_ref, acc, out_ref, tabs, send):
     ntab = atm_ref.shape[1] // LANES
     tiles = 2
     trips = n // (8 * tiles)
+    outer = n // n_inner
+    inner = n_inner // 8
     for f in range(NFIELD):
         for r in range(ntab):
             tabs[f * ntab + r] = jnp.broadcast_to(
@@ -103,10 +105,16 @@
             )
 
     def some(i, _):
-        turn = lax.rem(i + me // (8 * tiles), trips)
         todo = []
+        turns = []
         for u in range(tiles):
-            t = turn * tiles + u
+            m = i * tiles + u
+            up = lax.rem(m, outer)
+            across = m // outer + inner // 2 * lax.rem(up, 2) + up // 2
+            t = lax.rem(me // n_inner + up, outer) * inner + lax.rem(
+                lax.rem(me, n_inner) // 8 + across, inner
+            )
+            turns.append(t)
             for h in range(2):
                 lanes = slice(h * LANES, (h + 1) * LANES)
 
@@ -132,10 +140,11 @@
                 out_ref[pl.ds(t * 8 * SLAB + f * 2 + h, 8, stride=SLAB), :] = values[f] * weight
 
         def each(j, _):
-            send(turn * 8 * tiles + lax.rem(j + me, 8 * tiles))
+            for t in turns:
+                send(t * 8 + lax.rem(j + me, 8))
             return 0
 
-        lax.fori_loop(0, 8 * tiles, each, 0)
+        lax.fori_loop(0, 8, each, 0)
         return 0
 
     lax.fori_loop(0, trips, some, 0)
@@ -233,10 +242,20 @@
 
     barrier = pltpu.get_barrier_semaphore()
 
+    my_outer = lax.axis_index("grp")
+    my_inner = lax.axis_index("ocn")
+
     def greet(i, _):
-        pl.semaphore_signal(
-            barrier, inc=1, device_id=ident(lax.rem(me + i, n)), device_id_type=MESH
-        )
+        for g in range(n // n_inner):
+            other = (lax.rem(my_outer + g, n // n_inner), lax.rem(my_inner + i, n_inner))
+
+            def hello():
+                pl.semaphore_signal(barrier, inc=1, device_id=other, device_id_type=MESH)
+
+            if g == 0:
+                pl.when(i != 0)(hello)
+            else:
+                hello()
         return 0
 
     loads = [
@@ -252,7 +271,7 @@
     ]
     for load in loads:
         load.start()
-    lax.fori_loop(1, n, greet, 0, unroll=8)
+    lax.fori_loop(0, n_inner, greet, 0, unroll=4)
     loads[0].wait()
     rank_phase(n, dev_ref, ranks, 32)
 
@@ -305,7 +324,7 @@
         def _():
             slab_copy(d).start()
 
-    gather_phase(n, me, atm_ref, slots, packed, tabs, send_slab)
+    gather_phase(n, n_inner, me, atm_ref, slots, packed, tabs, send_slab)
     mine = pl.ds(pl.multiple_of(me * SLAB, 8), SLAB)
     own = pltpu.make_async_copy(packed.at[mine, :], received.at[mine, :], own_sem)
     own.start()

time: 47.5 us -> 46.3 us (0.975)
  Pallas kernels: 43.6 us -> 42.3 us
    pallas_call x1, Pallas kernels: 43.6 us -> 42.3 us  [per_device(): pl.pallas_call(functools.partial(move_kernel, n, n_inner, levels, cells),...]
where the time goes in v3:
time: 46.3 us; the launch traced here: 46 us
  Pallas kernels  42.3 us (91%)
  local copies, waits for them, and re-layouts  3.14 us (7%)
  between operations  0.65 us (1%)
    pallas_call x1, Pallas kernels, per_device(): pl.pallas_call(functools.partial(move_kernel, n, n_inner, levels, cells),...  42.3 us
    unnamed x4, local copies, waits for them, and re-layouts  3.14 us

profile of v3, /device:TPU:0, one launch (start us, length us, event | category | flops | bytes accessed | tf_op | source)
XLA Modules:
  0.0 46.0 jit_solution(5379241986537008326)
XLA Ops:
  0.6 42.3 %move.1 = (f32[4,80,1024]{2,1,0:T(8,128)}, f32[4,1024]{1,0:T(4,128)}) custom-call(s32[128,128]{1,0:T(8,128)} %bitcast.7, s32[128,128]{1,0:T(8,128)} %bitcast.8, s32[128,128]{1,0:T(8,128)} %bitcast.9, f32[128,128]{1,0:T(8,128)} %bitcast.10, f32[4,2048]{1,0:T(4,128)} %atm_hbm.1, f32[4,80,1024]{2,1,0:T(8,128)} %q_hbm.1, f32[6,1024]{1,0:T(8,128)} %coef_hbm.1, ...), custom_call_target="tpu_custom_call" | custom-call | tf_op jit(solution)/shard_map/move/pallas_call | solution.py:498
  42.9 0.0 copy-start
  42.9 2.5 %copy.16 = f32[4,80,1024]{2,1,0:T(8,128)} copy(f32[4,80,1024]{2,1,0:T(8,128)} %get-tuple-element.4) | data formatting | bytes 2621440
  45.4 0.0 copy-done
  45.4 0.6 %copy.17 = f32[4,1024]{1,0:T(4,128)} copy(f32[4,1024]{1,0:T(4,128)S(1)} %copy-done) | data formatting | bytes 32768
Async XLA Ops:
  42.9 2.5 %copy-start = (f32[4,1024]{1,0:T(4,128)S(1)}, f32[4,1024]{1,0:T(4,128)}, u32[]{:S(2)}) copy-start(f32[4,1024]{1,0:T(4,128)} %get-tuple-element.5) | copy-start | bytes 49156

commit v4 on v3

--- a/solution.py
+++ b/solution.py
@@ -225,13 +225,13 @@
     n, n_inner, levels, cells,
     dev_hbm, src_hbm, cell_hbm, w_hbm, atm_hbm,
     q_hbm, coef_hbm, nb_hbm, act_hbm, act8_hbm, bl8_hbm, kd_hbm, kv_hbm,
-    out_ref, surface_ref,
-    z_ref, e_ref, out_vmem,
+    z_out, e_out, r0_ref, flux_ref,
+    z_ref, e_ref,
     dev_ref, src_ref, cell_ref, w_ref, atm_ref,
     q_ref, coef_ref, nb_ref, act_ref, act8_ref, bl8_ref, kd_ref, kv_ref,
     ranks, slots, tabs, packed, received, surface_acc,
     halo, q1, split, sten_h, sten_l, rates, recip, total_ref,
-    halo_send, halo_recv, slab_send, slab_recv, own_sem, load_sem, out_sem,
+    halo_send, halo_recv, slab_send, slab_recv, own_sem, load_sem, out_sem, e_sem,
 ):
     tiles = cells // LANES
     me = lax.axis_index("grp") * n_inner + lax.axis_index("ocn")
@@ -416,16 +416,18 @@
     scatter_phase(n, received, surface_acc, 16)
     half = NFIELD * tiles
     surface = surface_acc[:half, :] + surface_acc[half:, :]
-    surface_acc[:half, :] = surface
-    for f in range(NFIELD):
-        for a in range(tiles):
-            r = f * tiles + a
-            surface_ref[f : f + 1, a * LANES : (a + 1) * LANES] = surface[r : r + 1, :]
-
-
-    def out_copy(g):
-        fields = pl.ds(2 * g, 2)
-        return pltpu.make_async_copy(out_vmem.at[fields], out_ref.at[fields], out_sem.at[g])
+    flux_ref[...] = surface
+
+    half_rows = 2 * levels * tiles
+
+    def z_copy(g):
+        at = pl.ds(g * half_rows, half_rows)
+        return pltpu.make_async_copy(z_ref.at[at, :], z_out.at[at, :], out_sem.at[g])
+
+    e_copy = pltpu.make_async_copy(e_ref, e_out, e_sem)
+    e_copy.start()
+    for c in range(2):
+        r0_ref[c * tiles : (c + 1) * tiles, :] = recip[pl.ds(c * levels * tiles, tiles), :]
 
     for g in range(2):
         advance(1, far, g)
@@ -443,38 +445,52 @@
             return tuple(after)
 
         lax.fori_loop(0, levels, lift, (nothing,) * 2, unroll=8)
-        below = []
-        for f in fields:
-            at = pl.ds(f * levels * tiles, tiles)
-            flux = surface_acc[f * tiles : (f + 1) * tiles, :]
-            top = z_ref[at, :] + flux * recip[pl.ds(g * levels * tiles, tiles), :]
-            z_ref[at, :] = top
-            below.append(top)
-
-        def drop(level, above):
-            own_at = pl.ds(pl.multiple_of((g * levels + level) * tiles, 8), tiles)
-            after = []
-            for f, carried in zip(fields, above):
-                at = pl.ds(pl.multiple_of((f * levels + level) * tiles, 8), tiles)
-                value = z_ref[at, :] + e_ref[own_at, :] * carried
-                z_ref[at, :] = value
-                after.append(value)
-            return tuple(after)
-
-        lax.fori_loop(1, levels, drop, tuple(below), unroll=8)
-        for f in fields:
-            for j in range(tiles):
-                out_vmem[f, :, j * LANES : (j + 1) * LANES] = z_ref[
-                    pl.ds(f * levels * tiles + j, levels, stride=tiles), :
-                ]
-        out_copy(g).start()
+        z_copy(g).start()
     for g in range(2):
-        out_copy(g).wait()
+        z_copy(g).wait()
+    e_copy.wait()
     arrived.wait_send()
     for step in range(ADV_STEPS):
         for side in range(2):
             for g in range(2):
                 halo_copy(step, side, g).wait_send()
+
+
+def finish_kernel(levels, cells, z_ref, e_ref, r0_ref, flux_ref, out_ref, surface_ref, state):
+    tiles = cells // LANES
+    g = pl.program_id(0)
+
+    @pl.when(g == 0)
+    def _():
+        for f in range(NFIELD):
+            for a in range(tiles):
+                r = f * tiles + a
+                surface_ref[f : f + 1, a * LANES : (a + 1) * LANES] = flux_ref[r : r + 1, :]
+
+    below = []
+    for f in range(2):
+        at = pl.ds(f * levels * tiles, tiles)
+        flux = flux_ref[pl.ds(pl.multiple_of((g * 2 + f) * tiles, 8), tiles), :]
+        top = z_ref[at, :] + flux * r0_ref[...]
+        state[at, :] = top
+        below.append(top)
+
+    def drop(level, above):
+        own_at = pl.ds(pl.multiple_of(level * tiles, 8), tiles)
+        after = []
+        for f in range(2):
+            at = pl.ds(pl.multiple_of((f * levels + level) * tiles, 8), tiles)
+            value = z_ref[at, :] + e_ref[own_at, :] * above[f]
+            state[at, :] = value
+            after.append(value)
+        return tuple(after)
+
+    lax.fori_loop(1, levels, drop, tuple(below), unroll=8)
+    for f in range(2):
+        for j in range(tiles):
+            out_ref[f, :, j * LANES : (j + 1) * LANES] = state[
+                pl.ds(f * levels * tiles + j, levels, stride=tiles), :
+            ]
 
 
 def vmem(count):
@@ -495,15 +511,19 @@
     pairs = pair_source.shape[0]
     wide = (pairs // LANES, LANES)
     rows_all = NFIELD * levels
-    return pl.pallas_call(
+    z, e, r0, flux = pl.pallas_call(
         functools.partial(move_kernel, n, n_inner, levels, cells),
-        out_shape=(shaped(NFIELD, levels, cells), shaped(NFIELD, cells)),
+        out_shape=(
+            shaped(rows_all * tiles, LANES),
+            shaped(2 * levels * tiles, LANES),
+            shaped(2 * tiles, LANES),
+            shaped(NFIELD * tiles, LANES),
+        ),
         in_specs=[pl.BlockSpec(memory_space=pltpu.HBM)] * 13,
-        out_specs=(pl.BlockSpec(memory_space=pltpu.HBM), vmem(1)[0]),
+        out_specs=tuple([pl.BlockSpec(memory_space=pltpu.HBM)] * 2 + vmem(2)),
         scratch_shapes=[
             pltpu.VMEM((rows_all * tiles, LANES), F32),
             pltpu.VMEM((2 * levels * tiles, LANES), F32),
-            pltpu.VMEM((NFIELD, levels, cells), F32),
             pltpu.VMEM(wide, I32),
             pltpu.VMEM(wide, I32),
             pltpu.VMEM(wide, I32),
@@ -538,6 +558,7 @@
             pltpu.SemaphoreType.DMA,
             pltpu.SemaphoreType.DMA((13,)),
             pltpu.SemaphoreType.DMA((2,)),
+            pltpu.SemaphoreType.DMA,
         ],
         compiler_params=pltpu.CompilerParams(
             vmem_limit_bytes=63 * 1024 * 1024, collective_id=0, has_side_effects=True
@@ -550,6 +571,25 @@
         active_levels.reshape(tiles, LANES), boundary_level.reshape(tiles, LANES),
         kpp_diff, kpp_visc,
     )
+    half = 2 * levels * tiles
+    return pl.pallas_call(
+        functools.partial(finish_kernel, levels, cells),
+        grid=(2,),
+        out_shape=(shaped(NFIELD, levels, cells), shaped(NFIELD, cells)),
+        in_specs=[
+            pl.BlockSpec((half, LANES), lambda g: (g, 0)),
+            pl.BlockSpec((levels * tiles, LANES), lambda g: (g, 0)),
+            pl.BlockSpec((tiles, LANES), lambda g: (g, 0)),
+            pl.BlockSpec((NFIELD * tiles, LANES), lambda g: (0, 0)),
+        ],
+        out_specs=(
+            pl.BlockSpec((2, levels, cells), lambda g: (g, 0, 0)),
+            pl.BlockSpec((NFIELD, cells), lambda g: (0, 0)),
+        ),
+        scratch_shapes=[pltpu.VMEM((half, LANES), F32)],
+        compiler_params=pltpu.CompilerParams(vmem_limit_bytes=63 * 1024 * 1024),
+        name="finish",
+    )(z, e, r0, flux)
 
 
 def solution(mesh):

time: 46.3 us -> 45.5 us (0.983)
  local copies, waits for them, and re-layouts: 3.14 us -> 0 us
  Pallas kernels: 42.3 us -> 44.7 us
    unnamed x4 -> x0, local copies, waits for them, and re-layouts: 3.14 us -> none
    pallas_call x0 -> x1, Pallas kernels: none -> 2.74 us  [per_device(): pl.pallas_call(functools.partial(finish_kernel, levels, cells), grid=(2,)...]
where the time goes in v4:
time: 45.5 us; the launch traced here: 45.3 us
  Pallas kernels  44.7 us (98%)
  between operations  0.64 us (1%)
    pallas_call x1, Pallas kernels, per_device(): pl.pallas_call(functools.partial(move_kernel, n, n_inner, levels, cells),...  42 us
    pallas_call x1, Pallas kernels, per_device(): pl.pallas_call(functools.partial(finish_kernel, levels, cells), grid=(2,)...  2.74 us

profile of v4, /device:TPU:0, one launch (start us, length us, event | category | flops | bytes accessed | tf_op | source)
XLA Modules:
  0.0 45.3 jit_solution(16473671376310463461)
XLA Ops:
  0.6 42.0 %move.1 = (f32[2560,128]{1,0:T(8,128)}, f32[1280,128]{1,0:T(8,128)}, f32[16,128]{1,0:T(8,128)}, f32[32,128]{1,0:T(8,128)}) custom-call(s32[128,128]{1,0:T(8,128)} %bitcast.7, s32[128,128]{1,0:T(8,128)} %bitcast.8, s32[128,128]{1,0:T(8,128)} %bitcast.9, f32[128,128]{1,0:T(8,128)} %bitcast.10, f32[4,2048]{1,0:T(4,128)} %atm_hbm.1, f32[4,80,1024]{2,1,0:T(8,128)} %q_hbm.1, ...), custom_call_target="tpu_custom_call" | custom-call | tf_op jit(solution)/shard_map/move/pallas_call | solution.py:514
  42.6 2.7 %finish.1 = (f32[4,80,1024]{2,1,0:T(8,128)}, f32[4,1024]{1,0:T(4,128)}) custom-call(f32[2560,128]{1,0:T(8,128)} %get-tuple-element.6.z_ref, f32[1280,128]{1,0:T(8,128)} %get-tuple-element.7.e_ref, f32[16,128]{1,0:T(8,128)} %get-tuple-element.8.r0_ref, f32[32,128]{1,0:T(8,128)} %get-tuple-element.9.flux_ref), custom_call_target="tpu_custom_call" | custom-call | tf_op jit(solution)/shard_map/finish/pallas_call | solution.py:575

commit v5 on v4

--- a/solution.py
+++ b/solution.py
@@ -522,7 +522,7 @@
         in_specs=[pl.BlockSpec(memory_space=pltpu.HBM)] * 13,
         out_specs=tuple([pl.BlockSpec(memory_space=pltpu.HBM)] * 2 + vmem(2)),
         scratch_shapes=[
-            pltpu.VMEM((rows_all * tiles, LANES), F32),
+            pltpu.VMEM((rows_all * tiles + 8, LANES), F32),
             pltpu.VMEM((2 * levels * tiles, LANES), F32),
             pltpu.VMEM(wide, I32),
             pltpu.VMEM(wide, I32),
@@ -540,7 +540,7 @@
             pltpu.VMEM(wide, F32),
             pltpu.VMEM((5 * n, SLOTS), F32),
             pltpu.VMEM((NFIELD * atm_flux.shape[1] // LANES, 8, LANES), F32),
-            pltpu.VMEM((n * SLAB, LANES), F32),
+            pltpu.VMEM((n * SLAB + SLAB, LANES), F32),
             pltpu.VMEM((n * SLAB, LANES), F32),
             pltpu.VMEM((2 * NFIELD * tiles, LANES), F32),
             pltpu.VMEM((ADV_STEPS, 2, NFIELD, levels, HW), F32),
@@ -548,7 +548,7 @@
             pltpu.VMEM((2 * rows_all, cells + 2 * HW), BF16),
             pltpu.VMEM((cells // BLOCK, BAND, BLOCK), BF16),
             pltpu.VMEM((cells // BLOCK, BAND, BLOCK), BF16),
-            pltpu.VMEM((2 * levels * tiles, LANES), F32),
+            pltpu.VMEM((2 * levels * tiles + 8, LANES), F32),
             pltpu.VMEM((2 * levels * tiles, LANES), F32),
             pltpu.VMEM((8, cells), F32),
             pltpu.SemaphoreType.DMA((ADV_STEPS, 2, 2)),
@@ -586,7 +586,7 @@
             pl.BlockSpec((2, levels, cells), lambda g: (g, 0, 0)),
             pl.BlockSpec((NFIELD, cells), lambda g: (0, 0)),
         ),
-        scratch_shapes=[pltpu.VMEM((half, LANES), F32)],
+        scratch_shapes=[pltpu.VMEM((half + 8, LANES), F32)],
         compiler_params=pltpu.CompilerParams(vmem_limit_bytes=63 * 1024 * 1024),
         name="finish",
     )(z, e, r0, flux)

time: 45.5 us -> 45.5 us (level)
  no operation moved by 1% of the time
where the time goes in v5:
time: 45.5 us; the launch traced here: 45.4 us
  Pallas kernels  44.7 us (98%)
  between operations  0.64 us (1%)
    pallas_call x1, Pallas kernels, per_device(): pl.pallas_call(functools.partial(move_kernel, n, n_inner, levels, cells),...  42 us
    pallas_call x1, Pallas kernels, per_device(): pl.pallas_call(functools.partial(finish_kernel, levels, cells), grid=(2,)...  2.74 us

profile of v5, /device:TPU:0, one launch (start us, length us, event | category | flops | bytes accessed | tf_op | source)
XLA Modules:
  0.0 45.4 jit_solution(1452559856061501095)
XLA Ops:
  0.6 42.0 %move.1 = (f32[2560,128]{1,0:T(8,128)}, f32[1280,128]{1,0:T(8,128)}, f32[16,128]{1,0:T(8,128)}, f32[32,128]{1,0:T(8,128)}) custom-call(s32[128,128]{1,0:T(8,128)} %bitcast.7, s32[128,128]{1,0:T(8,128)} %bitcast.8, s32[128,128]{1,0:T(8,128)} %bitcast.9, f32[128,128]{1,0:T(8,128)} %bitcast.10, f32[4,2048]{1,0:T(4,128)} %atm_hbm.1, f32[4,80,1024]{2,1,0:T(8,128)} %q_hbm.1, ...), custom_call_target="tpu_custom_call" | custom-call | tf_op jit(solution)/shard_map/move/pallas_call | solution.py:514
  42.6 2.7 %finish.1 = (f32[4,80,1024]{2,1,0:T(8,128)}, f32[4,1024]{1,0:T(4,128)}) custom-call(f32[2560,128]{1,0:T(8,128)} %get-tuple-element.6.z_ref, f32[1280,128]{1,0:T(8,128)} %get-tuple-element.7.e_ref, f32[16,128]{1,0:T(8,128)} %get-tuple-element.8.r0_ref, f32[32,128]{1,0:T(8,128)} %get-tuple-element.9.flux_ref), custom_call_target="tpu_custom_call" | custom-call | tf_op jit(solution)/shard_map/finish/pallas_call | solution.py:575
